TPU v7x, 32 devices: a whole 2x2x4 slice. The times are simulated.
32 devices in a mesh: cam: 4 (over x, core), pt: 8 (over z, y).
Axes of the slice: x: 2, y: 2, z: 4, core: 2. Of those that a mesh axis runs over, the one named last changes fastest.
Arguments:
- right_side: float32 [9, 65536], P(None, ('cam', 'pt')), may hold values from -6 to 6
- cam_damping: float32 [9, 65536], P(None, ('cam', 'pt')), may hold values from 0.5 to 4
- point_damping: float32 [524288], P('pt'), may hold values from 0.1 to 1
- block_ids: int32 [4, 8, 64], P('cam', 'pt'), may hold values from 0 to 255, as said below
- slab_ids: int32 [4, 8, 64], P('cam', 'pt'), may hold values from 0 to 15
- cam_index: int32 [4, 8, 64, 4096], P('cam', 'pt'), may hold values from 0 to 63
- cam_jacobian: bfloat16 [4, 8, 64, 18, 4096], P('cam', 'pt'), may hold values from -0.59765625 to 0.59765625
- point_jacobian: bfloat16 [4, 8, 64, 6, 4096], P('cam', 'pt'), may hold values from -1.796875 to 1.796875
- pair_count: int32 [4, 8], P('cam', 'pt'), may hold values from 16 to 64, as said below
Outputs:
- solution: float32 [9, 65536], P(None, ('cam', 'pt'))
- residual: float32 [9, 65536], P(None, ('cam', 'pt'))
Inputs may be any that keep to these rules, and one draw needn't show every extreme that they name: pair_count is 64 divided by a whole number from 1 to 4, rounded down; at least one device has all 64 slots used in every draw. The owner of a block is block_ids // 32; in every device's list at most 16 slots name blocks of one owner, and in every list some owner is named by exactly 16 slots.
All inputs are finite; a program needn't handle non-finite values.
Results may differ from a plain program's by a relative error of at most 0.0003.
Values sent between devices are 32-bit elements; how exact they have to be, the bound alone decides.
A program may use at most 128 MiB of HBM per device.

v0:
```python
import jax
import jax.numpy as jnp
from jax import lax
from jax.sharding import PartitionSpec as P

BLOCK = 64
ITERS = 2
HIGH = lax.Precision.HIGHEST


def hessian_terms(pt_jac):
    combos = [(0, 0), (0, 1), (0, 2), (1, 1), (1, 2), (2, 2)]
    return jnp.stack(
        [
            jnp.sum(pt_jac[:, :, first].astype(jnp.float32) * pt_jac[:, :, second], axis=1)
            for first, second in combos
        ],
        axis=1,
    )


def collect(selector, terms):
    summed = jnp.einsum("ps,pkn->ksn", selector, terms, precision=HIGH)
    return summed.reshape(terms.shape[1], -1)


def invert_points(hess, damping):
    entry_xx = hess[0] + damping
    entry_xy = hess[1]
    entry_xz = hess[2]
    entry_yy = hess[3] + damping
    entry_yz = hess[4]
    entry_zz = hess[5] + damping
    cof_xx = entry_yy * entry_zz - entry_yz * entry_yz
    cof_xy = entry_xz * entry_yz - entry_xy * entry_zz
    cof_xz = entry_xy * entry_yz - entry_xz * entry_yy
    cof_yy = entry_xx * entry_zz - entry_xz * entry_xz
    cof_yz = entry_xy * entry_xz - entry_xx * entry_yz
    cof_zz = entry_xx * entry_yy - entry_xy * entry_xy
    determinant = entry_xx * cof_xx + entry_xy * cof_xy + entry_xz * cof_xz
    return jnp.stack([cof_xx, cof_xy, cof_xz, cof_yy, cof_yz, cof_zz]) / determinant


def apply_inverse(inverse, vector):
    out_x = inverse[0] * vector[0] + inverse[1] * vector[1] + inverse[2] * vector[2]
    out_y = inverse[1] * vector[0] + inverse[3] * vector[1] + inverse[4] * vector[2]
    out_z = inverse[2] * vector[0] + inverse[4] * vector[1] + inverse[5] * vector[2]
    return jnp.stack([out_x, out_y, out_z])


def select_cameras(picked, index_here):
    pairs = picked.shape[0]

    def select_per_group(pieces):
        picked_group, index_group = pieces
        one_hot = (
            index_group[:, :, None] == jnp.arange(BLOCK, dtype=jnp.int32)[None, None, :]
        ).astype(jnp.float32)
        return jnp.einsum("gkb,gnb->gkn", picked_group, one_hot, precision=HIGH)

    grouped = lax.map(
        select_per_group,
        (picked.reshape(pairs // 8, 8, 9, BLOCK), index_here.reshape(pairs // 8, 8, -1)),
    )
    return grouped.reshape(pairs, 9, -1)


def project(cam_panel, blocks_here, index_here, cam_jac):
    grouped = cam_panel.reshape(9, -1, BLOCK).transpose(1, 0, 2)
    picked = grouped[blocks_here]
    at_camera = select_cameras(picked, index_here)
    return jnp.sum(cam_jac * at_camera[:, None], axis=2)


def camera_sums(pushed, index_here):
    pairs = pushed.shape[0]

    def camera_per_group(pieces):
        pushed_group, index_group = pieces
        one_hot = (
            index_group[:, :, None] == jnp.arange(BLOCK, dtype=jnp.int32)[None, None, :]
        ).astype(jnp.float32)
        return jnp.einsum("gkn,gnb->gkb", pushed_group, one_hot, precision=HIGH)

    grouped = lax.map(
        camera_per_group,
        (pushed.reshape(pairs // 8, 8, 9, -1), index_here.reshape(pairs // 8, 8, -1)),
    )
    return grouped.reshape(pairs, 9, BLOCK)


def dot_whole(first, second):
    return lax.psum(jnp.sum(first * second), "cam")


def per_device(
    right_side,
    cam_damping,
    point_damping,
    block_ids,
    slab_ids,
    cam_index,
    cam_jacobian,
    point_jacobian,
    pair_count,
):
    pairs = block_ids.shape[2]
    slab_len = cam_index.shape[3]
    slabs = point_damping.shape[0] // slab_len
    cam_dev = right_side.shape[1]
    owners_count = lax.axis_size("pt")
    blk_owner = cam_dev // BLOCK
    blk_group = blk_owner * owners_count
    blocks_here = block_ids.reshape(pairs)
    slabs_here = slab_ids.reshape(pairs)
    index_here = cam_index.reshape(pairs, slab_len)
    cam_jac = cam_jacobian.reshape(pairs, 2, 9, slab_len)
    pt_jac = point_jacobian.reshape(pairs, 2, 3, slab_len)
    live_pairs = (jnp.arange(pairs, dtype=jnp.int32) < pair_count.reshape(())).astype(jnp.float32)
    slab_onehot = (slabs_here[:, None] == jnp.arange(slabs, dtype=jnp.int32)[None, :]).astype(
        jnp.float32
    )
    selector = slab_onehot * live_pairs[:, None]
    block_onehot = (blocks_here[:, None] == jnp.arange(blk_group, dtype=jnp.int32)[None, :]).astype(
        jnp.float32
    )
    hess_local = collect(selector, hessian_terms(pt_jac))
    inverse = invert_points(lax.psum(hess_local, "cam"), point_damping)
    residual, damping_here = (
        lax.all_gather(right_side, "pt", axis=1, tiled=True),
        lax.all_gather(cam_damping, "pt", axis=1, tiled=True),
    )
    solution = jnp.zeros_like(residual)
    direction = residual
    norm_now = dot_whole(residual, residual)
    for iteration in range(ITERS):
        projected = project(direction, blocks_here, index_here, cam_jac)
        pulled = jnp.sum(pt_jac * projected[:, :, None], axis=1)
        eliminated = apply_inverse(inverse, lax.psum(collect(selector, pulled), "cam")).reshape(
            3, slabs, slab_len
        )
        pulled_back = jnp.einsum("ps,ksn->pkn", slab_onehot, eliminated, precision=HIGH)
        miss = projected - jnp.sum(pt_jac * pulled_back[:, None], axis=2)
        pushed = jnp.sum(cam_jac * miss[:, :, None], axis=1)
        group_sum = jnp.einsum(
            "pg,pkb->kgb",
            block_onehot,
            camera_sums(pushed, index_here) * live_pairs[:, None, None],
            precision=HIGH,
        )
        image = damping_here * direction + lax.psum(group_sum.reshape(9, blk_group * BLOCK), "pt")
        step_size = norm_now / dot_whole(direction, image)
        solution = solution + step_size * direction
        residual = residual - step_size * image
        norm_next = dot_whole(residual, residual)
        direction = residual + norm_next / norm_now * direction
        norm_now = norm_next
    start = lax.axis_index("pt") * cam_dev
    solution = lax.dynamic_slice_in_dim(solution, start, cam_dev, 1)
    residual = lax.dynamic_slice_in_dim(residual, start, cam_dev, 1)
    return (solution, residual)


def solution(mesh):
    in_specs = (
        P(None, ("cam", "pt")),
        P(None, ("cam", "pt")),
        P("pt"),
        P("cam", "pt", None),
        P("cam", "pt", None),
        P("cam", "pt", None, None),
        P("cam", "pt", None, None, None),
        P("cam", "pt", None, None, None),
        P("cam", "pt"),
    )
    out_specs = (P(None, ("cam", "pt")), P(None, ("cam", "pt")))
    return jax.shard_map(
        per_device, mesh=mesh, in_specs=in_specs, out_specs=out_specs, check_vma=False
    )
```

profile of v0, /device:TPU:0, one launch (start us, length us, event | category | flops | bytes accessed | tf_op | source)
XLA Modules:
  0.0 737.0 jit_solution(18072257541709590716)
XLA Ops:
  18.2 34.7 %all_gather.6 = f32[9,16384]{1,0:T(8,128)S(1)} all-gather(f32[9,2048]{1,0:T(8,128)S(1)} %copy-done.11), channel_id=1, replica_groups=mesh['cam'=4,'pt'=8] {'pt'}, dimensions={1}, use_global_device_ids=true | all-gather | bytes 663552 | tf_op jit(solution)/shard_map/all_gather | solution.py:130
  57.7 7.8 %broadcast.107.clone = f32[8,8,9,4096]{3,2,1,0:T(8,128)} broadcast(f32[]{:T(128)} %constant.49.clone.1), dimensions={} | broadcast | bytes 9437188 | tf_op jit(solution)/shard_map/broadcast.5
  65.6 39.4 %while.40 = (s32[]{:T(128)}, f32[8,8,9,4096]{3,2,1,0:T(8,128)}, f32[8,8,9,64]{3,2,1,0:T(8,128)S(1)}, s32[8,8,4096]{2,1,0:T(8,128)}, s32[]{:T(128)}) while((s32[]{:T(128)}, f32[8,8,9,4096]{3,2,1,0:T(8,128)}, f32[8,8,9,64]{3,2,1,0:T(8,128)S(1)}, s32[8,8,4096]{2,1,0:T(8,128)}, s32[]{:T(128)}) %tuple.115), condition=%wide.region_3.0_spmd, body=%wide.region_2.0_spmd.sunk | while | flops 228589568 | bytes 2556993 | solution.py:61
  104.9 14.9 %copy.26 = f32[64,9,4096]{2,0,1:T(8,128)} copy(f32[64,9,4096]{2,1,0:T(8,128)} %bitcast.161) | data formatting | bytes 18874368 | tf_op jit(solution)/shard_map/mul | solution.py:72
  119.8 8.0 %fusion.22 = f32[64,2,4096]{2,0,1:T(8,128)S(1)} fusion(bf16[64,2,9,4096]{3,0,2,1:T(8,128)(2,1)} %bitcast.152, f32[64,9,4096]{2,0,1:T(8,128)} %copy.26), kind=kLoop, calls=%fused_computation.40 | loop fusion | flops 13631488 | bytes 20971520 | tf_op jit(solution)/shard_map/reduce_sum | solution.py:72
  132.5 69.4 %all-reduce.13.cloned.1.call-done = (f32[6,65536]{1,0:T(8,128)}, f32[3,65536]{1,0:T(4,128)}) async-done(((f32[6,65536]{1,0:T(8,128)}, f32[3,65536]{1,0:T(4,128)}), (f32[6,65536]{1,0:T(8,128)}, f32[3,65536]{1,0:T(4,128)})) %all-reduce.13.cloned.1.call-update) | async-done | bytes 2359312 | tf_op jit(solution)/shard_map/psum | solution.py:128
  201.9 6.8 fusion.84
  211.5 6.5 stack.79
  235.7 11.2 %fusion.23 = f32[64,9,4096]{2,0,1:T(8,128)} fusion(bf16[64,2,9,4096]{3,0,2,1:T(8,128)(2,1)} %bitcast.153, f32[64,2,4096]{2,0,1:T(8,128)} %sub.44), kind=kLoop, calls=%fused_computation.41 | loop fusion | flops 11796480 | bytes 20971520 | tf_op jit(solution)/shard_map/reduce_sum | solution.py:144
  247.7 58.1 %while.41 = (s32[]{:T(128)}, f32[8,8,9,64]{3,2,1,0:T(8,128)}, f32[8,8,9,4096]{3,1,0,2:T(8,128)}, s32[8,8,4096]{2,1,0:T(8,128)}, s32[]{:T(128)}) while((s32[]{:T(128)}, f32[8,8,9,64]{3,2,1,0:T(8,128)}, f32[8,8,9,4096]{3,1,0,2:T(8,128)}, s32[8,8,4096]{2,1,0:T(8,128)}, s32[]{:T(128)}) %tuple.111), condition=%wide.region_17.18_spmd, body=%wide.region_16.17_spmd.sunk | while | flops 228589568 | bytes 3998277 | solution.py:85
  313.7 36.7 %all_gather.7 = f32[9,16384]{1,0:T(8,128)} all-gather(f32[9,2048]{1,0:T(8,128)S(1)} %copy-done.12), channel_id=1, replica_groups=mesh['cam'=4,'pt'=8] {'pt'}, dimensions={1}, use_global_device_ids=true | all-gather | bytes 663552 | tf_op jit(solution)/shard_map/all_gather | solution.py:131
  350.4 49.2 %all-reduce.7.cloned.1.call-done = f32[9,16384]{1,0:T(8,128)} async-done(((f32[9,16384]{1,0:T(8,128)}), f32[9,16384]{1,0:T(8,128)}) %all-reduce.7.cloned.1.call-update) | async-done | bytes 589840 | tf_op jit(solution)/shard_map/psum | solution.py:151
  402.3 7.1 all-reduce
  414.5 6.6 psum.68
  434.1 7.8 %broadcast.107 = f32[8,8,9,4096]{3,2,1,0:T(8,128)} broadcast(f32[]{:T(128)} %constant.49.clone.1), dimensions={} | broadcast | bytes 9437188 | tf_op jit(solution)/shard_map/broadcast.5
  441.9 45.9 %while.42 = (s32[]{:T(128)}, f32[8,8,9,4096]{3,2,1,0:T(8,128)}, f32[8,8,9,64]{3,2,1,0:T(8,128)}, s32[8,8,4096]{2,1,0:T(8,128)}, s32[]{:T(128)}) while((s32[]{:T(128)}, f32[8,8,9,4096]{3,2,1,0:T(8,128)}, f32[8,8,9,64]{3,2,1,0:T(8,128)}, s32[8,8,4096]{2,1,0:T(8,128)}, s32[]{:T(128)}) %tuple.114), condition=%wide.region_24.25_spmd, body=%wide.region_23.24_spmd.sunk | while | flops 228589568 | bytes 2556993 | solution.py:61
  487.8 14.9 %copy.31 = f32[64,9,4096]{2,0,1:T(8,128)} copy(f32[64,9,4096]{2,1,0:T(8,128)} %bitcast.162) | data formatting | bytes 18874368 | tf_op jit(solution)/shard_map/mul | solution.py:72
  502.6 7.6 %fusion.24 = f32[64,2,4096]{2,0,1:T(8,128)S(1)} fusion(bf16[64,2,9,4096]{3,0,2,1:T(8,128)(2,1)} %bitcast.154, f32[64,9,4096]{2,0,1:T(8,128)} %copy.31), kind=kLoop, calls=%fused_computation.42 | loop fusion | flops 13631488 | bytes 20971520 | tf_op jit(solution)/shard_map/reduce_sum | solution.py:72
  514.9 35.6 %all-reduce.9.cloned.1.call-done = f32[3,65536]{1,0:T(4,128)} async-done(((f32[3,65536]{1,0:T(4,128)}), f32[3,65536]{1,0:T(4,128)}) %all-reduce.9.cloned.1.call-update) | async-done | bytes 786448 | tf_op jit(solution)/shard_map/psum | solution.py:139
  550.5 11.2 %add_reduce_fusion.2 = (f32[65536]{0:T(1024)}, f32[65536]{0:T(1024)}, f32[65536]{0:T(1024)S(1)}) fusion(f32[6,65536]{1,0:T(8,128)} %copy-done.7, f32[3,65536]{1,0:T(4,128)} %all-reduce.9.cloned.1.call-done), kind=kLoop, calls=%fused_computation.102 | loop fusion | flops 983040 | bytes 3145728 | tf_op jit(solution)/shard_map/add | solution.py:45
  570.2 10.6 %fusion.25 = f32[64,9,4096]{2,0,1:T(8,128)} fusion(bf16[64,2,9,4096]{3,0,2,1:T(8,128)(2,1)} %bitcast.155, f32[64,2,4096]{2,0,1:T(8,128)S(1)} %sub.46), kind=kLoop, calls=%fused_computation.43 | loop fusion | flops 11796480 | bytes 20971520 | tf_op jit(solution)/shard_map/reduce_sum | solution.py:144
  580.9 53.1 %while.43 = (s32[]{:T(128)}, f32[8,8,9,64]{3,2,1,0:T(8,128)S(1)}, f32[8,8,9,4096]{3,1,0,2:T(8,128)}, s32[8,8,4096]{2,1,0:T(8,128)}, s32[]{:T(128)}) while((s32[]{:T(128)}, f32[8,8,9,64]{3,2,1,0:T(8,128)S(1)}, f32[8,8,9,4096]{3,1,0,2:T(8,128)}, s32[8,8,4096]{2,1,0:T(8,128)}, s32[]{:T(128)}) %tuple.113), condition=%wide.region_31.32_spmd, body=%wide.region_30.31_spmd.sunk | while | flops 228589568 | bytes 3997769 | solution.py:85
  638.8 79.0 %all-reduce.11.cloned.1.call-done = f32[9,16384]{1,0:T(8,128)} async-done(((f32[9,16384]{1,0:T(8,128)}), f32[9,16384]{1,0:T(8,128)}) %all-reduce.11.cloned.1.call-update) | async-done | bytes 589840 | tf_op jit(solution)/shard_map/psum | solution.py:151
  719.9 7.1 psum.71
  (173 shorter events, 284.9 us)
Async XLA Ops:
  7.2 194.7 %all-reduce.13.cloned.1.call-start = ((), (), s32[]{:S(2)}) async-start(), calls=%async_computation.3 | async-start | bytes 6291456 | tf_op jit(solution)/shard_map/psum | solution.py:128
  11.9 0.7 copy-start.13
  16.0 2.3 copy-start.11
  18.2 37.3 %copy-start.14 = (s32[1,1,64]{2,1,0:T(1,128)S(1)}, s32[1,1,64]{2,1,0:T(1,128)}, u32[]{:S(2)}) copy-start(s32[1,1,64]{2,1,0:T(1,128)} %param.20) | copy-start | bytes 772
  53.0 4.8 copy-start.1
  119.8 8.0 %copy-start = (bf16[1,1,64,6,4096]{4,2,3,1,0:T(8,128)(2,1)S(1)}, bf16[1,1,64,6,4096]{4,2,3,1,0:T(8,128)(2,1)}, u32[]{:S(2)}) copy-start(bf16[1,1,64,6,4096]{4,2,3,1,0:T(8,128)(2,1)} %param.24) | copy-start | bytes 9437188
  127.8 1.4 copy-start.2
  132.5 267.1 %all-reduce.7.cloned.1.call-start = ((), (), s32[]{:S(2)}) async-start(), calls=%async_computation | async-start | bytes 2097152 | tf_op jit(solution)/shard_map/psum | solution.py:151
  201.9 8.7 %copy-start.9 = (f32[65536]{0:T(1024)S(1)}, f32[65536]{0:T(1024)}, u32[]{:S(2)}) copy-start(f32[65536]{0:T(1024)} %param.19) | copy-start | bytes 786436
  218.0 3.3 copy-start.10
  220.0 1.3 copy-start.7
  232.6 1.6 copy-start.3
  308.4 5.3 copy-start.12
  313.6 236.8 %all-reduce.9.cloned.1.call-start = ((), (), s32[]{:S(2)}) async-start(), calls=%async_computation.1 | async-start | bytes 2097152 | tf_op jit(solution)/shard_map/psum | solution.py:139
  510.2 1.4 copy-start.4
  514.9 202.9 %all-reduce.11.cloned.1.call-start = ((), (), s32[]{:S(2)}) async-start(), calls=%async_computation.2 | async-start | bytes 2097152 | tf_op jit(solution)/shard_map/psum | solution.py:151
  568.4 1.6 copy-start.5
  634.2 83.6 %copy-start.6 = (f32[9,16384]{1,0:T(8,128)S(1)}, f32[9,16384]{1,0:T(8,128)}, u32[]{:S(2)}) copy-start(f32[9,16384]{1,0:T(8,128)} %all_gather.7) | copy-start | bytes 1769476
  634.2 83.6 %copy-start.8 = (f32[9,16384]{1,0:T(8,128)S(1)}, f32[9,16384]{1,0:T(8,128)}, u32[]{:S(2)}) copy-start(f32[9,16384]{1,0:T(8,128)} %multiply_add_fusion.1) | copy-start | bytes 1769476
Sparse Core Ops, SparseCore 0:
  132.6 69.2 all-reduce.12
  313.8 85.7 all-reduce.6
  515.0 35.4 all-reduce.8
  638.9 78.8 all-reduce.10
where the time goes:
time: 747 us; the launch traced here: 737 us
  waiting for transfers between devices  233 us (31%)
  matrix products  159 us (21%)
  local copies, waits for them, and re-layouts  153 us (20%)
  blocking collectives  92.2 us (12%)
  other arithmetic  79.7 us (11%)
  between operations  19.2 us (3%)
    psum x2, waiting for transfers between devices, per_device(): lax.psum(group_sum.reshape(9, blk_group * BLOCK), 'pt')  128 us
    dot_general x16, matrix products, camera_per_group(): return jnp.einsum('gkn,gnb->gkb', pushed_group, one_hot, precision=HIGH)  74.6 us
    dot_general x16, matrix products, select_per_group(): return jnp.einsum('gkb,gnb->gkn', picked_group, one_hot, precision=HIGH)  70.4 us
    psum x1, waiting for transfers between devices, per_device(): inverse = invert_points(lax.psum(hess_local, 'cam'), point_damping)  69.4 us
    all_gather x1, blocking collectives, per_device(): lax.all_gather(cam_damping, 'pt', axis=1, tiled=True)  36.7 us
    psum x1, waiting for transfers between devices, per_device(): lax.psum(collect(selector, pulled), 'cam')  35.6 us
    all_gather x1, blocking collectives, per_device(): lax.all_gather(right_side, 'pt', axis=1, tiled=True)  34.7 us
    mul x2, local copies, waits for them, and re-layouts, project(): return jnp.sum(cam_jac * at_camera[:, None], axis=2)  29.7 us
  transfers between devices with their start and end apart: 4, of which 4 were waited for; matrix products, arithmetic and copies ran while one was open for 0% of the time, Pallas kernels for 0%

commit v1 on v0

--- a/solution.py
+++ b/solution.py
@@ -6,6 +6,11 @@
 BLOCK = 64
 ITERS = 2
 HIGH = lax.Precision.HIGHEST
+
+
+def summed_here(x, name):
+    shards = lax.all_gather(x, name)
+    return jnp.sum(shards, axis=0)
 
 
 def hessian_terms(pt_jac):
@@ -148,7 +153,9 @@
             camera_sums(pushed, index_here) * live_pairs[:, None, None],
             precision=HIGH,
         )
-        image = damping_here * direction + lax.psum(group_sum.reshape(9, blk_group * BLOCK), "pt")
+        image = damping_here * direction + summed_here(
+            group_sum.reshape(9, blk_group * BLOCK), "pt"
+        )
         step_size = norm_now / dot_whole(direction, image)
         solution = solution + step_size * direction
         residual = residual - step_size * image

time: 747 us -> 843 us (1.13)
  waiting for transfers between devices: 233 us -> 321 us
  other arithmetic: 79.7 us -> 88.6 us
    all_gather x0 -> x2, waiting for transfers between devices: none -> 217 us  [summed_here(): shards = lax.all_gather(x, name)]
    psum x2 -> x0, waiting for transfers between devices: 128 us -> none  [per_device(): lax.psum(group_sum.reshape(9, blk_group * BLOCK), 'pt')]
    reduce_sum x0 -> x2, other arithmetic: none -> 8.96 us  [summed_here(): return jnp.sum(shards, axis=0)]
    another operation x4 -> x6, local copies, waits for them, and re-layouts: 16.5 us -> 20.7 us
where the time goes in v1:
time: 843 us; the launch traced here: 833 us
  waiting for transfers between devices  321 us (38%)
  matrix products  159 us (19%)
  local copies, waits for them, and re-layouts  151 us (18%)
  blocking collectives  93.4 us (11%)
  other arithmetic  88.6 us (11%)
  between operations  19 us (2%)
    all_gather x2, waiting for transfers between devices, summed_here(): shards = lax.all_gather(x, name)  217 us
    dot_general x16, matrix products, camera_per_group(): return jnp.einsum('gkn,gnb->gkb', pushed_group, one_hot, precision=HIGH)  74.6 us
    dot_general x16, matrix products, select_per_group(): return jnp.einsum('gkb,gnb->gkn', picked_group, one_hot, precision=HIGH)  70.4 us
    psum x1, waiting for transfers between devices, per_device(): inverse = invert_points(lax.psum(hess_local, 'cam'), point_damping)  69.4 us
    all_gather x1, blocking collectives, per_device(): lax.all_gather(cam_damping, 'pt', axis=1, tiled=True)  38.6 us
    all_gather x1, blocking collectives, per_device(): lax.all_gather(right_side, 'pt', axis=1, tiled=True)  34.7 us
    psum x1, waiting for transfers between devices, per_device(): lax.psum(collect(selector, pulled), 'cam')  34.1 us
    mul x2, local copies, waits for them, and re-layouts, project(): return jnp.sum(cam_jac * at_camera[:, None], axis=2)  29.7 us
  transfers between devices with their start and end apart: 4, of which 4 were waited for; matrix products, arithmetic and copies ran while one was open for 0% of the time, Pallas kernels for 0%

profile of v1, /device:TPU:0, one launch (start us, length us, event | category | flops | bytes accessed | tf_op | source)
XLA Modules:
  0.0 832.9 jit_solution(9699115200828610479)
XLA Ops:
  18.2 34.7 %all_gather.12 = f32[9,16384]{1,0:T(8,128)S(1)} all-gather(f32[9,2048]{1,0:T(8,128)S(1)} %copy-done.11), channel_id=1, replica_groups=mesh['cam'=4,'pt'=8] {'pt'}, dimensions={1}, use_global_device_ids=true | all-gather | bytes 663552 | tf_op jit(solution)/shard_map/all_gather | solution.py:135
  57.7 7.8 broadcast.107.clone
  65.6 39.4 %while.40 = (s32[]{:T(128)}, f32[8,8,9,4096]{3,2,1,0:T(8,128)}, f32[8,8,9,64]{3,2,1,0:T(8,128)S(1)}, s32[8,8,4096]{2,1,0:T(8,128)}, s32[]{:T(128)}) while((s32[]{:T(128)}, f32[8,8,9,4096]{3,2,1,0:T(8,128)}, f32[8,8,9,64]{3,2,1,0:T(8,128)S(1)}, s32[8,8,4096]{2,1,0:T(8,128)}, s32[]{:T(128)}) %tuple.115), condition=%wide.region_3.0_spmd, body=%wide.region_2.0_spmd.sunk | while | flops 228589568 | bytes 2556993 | solution.py:66
  105.0 14.9 %copy.26 = f32[64,9,4096]{2,0,1:T(8,128)} copy(f32[64,9,4096]{2,1,0:T(8,128)} %bitcast.161) | data formatting | bytes 18874368 | tf_op jit(solution)/shard_map/mul | solution.py:77
  119.9 8.1 fusion.22
  132.7 69.4 %all-reduce.7.cloned.1.call-done = (f32[6,65536]{1,0:T(8,128)}, f32[3,65536]{1,0:T(4,128)}) async-done(((f32[6,65536]{1,0:T(8,128)}, f32[3,65536]{1,0:T(4,128)}), (f32[6,65536]{1,0:T(8,128)}, f32[3,65536]{1,0:T(4,128)})) %all-reduce.7.cloned.1.call-update) | async-done | bytes 2359312 | tf_op jit(solution)/shard_map/psum | solution.py:133
  202.0 6.8 fusion.84
  211.7 6.6 stack.79
  236.0 11.2 %fusion.23 = f32[64,9,4096]{2,0,1:T(8,128)} fusion(bf16[64,2,9,4096]{3,0,2,1:T(8,128)(2,1)} %bitcast.153, f32[64,2,4096]{2,0,1:T(8,128)} %sub.44), kind=kLoop, calls=%fused_computation.41 | loop fusion | flops 11796480 | bytes 20971520 | tf_op jit(solution)/shard_map/reduce_sum | solution.py:149
  248.0 58.1 %while.41 = (s32[]{:T(128)}, f32[8,8,9,64]{3,2,1,0:T(8,128)}, f32[8,8,9,4096]{3,1,0,2:T(8,128)}, s32[8,8,4096]{2,1,0:T(8,128)}, s32[]{:T(128)}) while((s32[]{:T(128)}, f32[8,8,9,64]{3,2,1,0:T(8,128)}, f32[8,8,9,4096]{3,1,0,2:T(8,128)}, s32[8,8,4096]{2,1,0:T(8,128)}, s32[]{:T(128)}) %tuple.111), condition=%wide.region_17.18_spmd, body=%wide.region_16.17_spmd.sunk | while | flops 228589568 | bytes 3998277 | solution.py:90
  314.0 38.6 %all_gather.13 = f32[9,16384]{1,0:T(8,128)} all-gather(f32[9,2048]{1,0:T(8,128)S(1)} %copy-done.12), channel_id=1, replica_groups=mesh['cam'=4,'pt'=8] {'pt'}, dimensions={1}, use_global_device_ids=true | all-gather | bytes 663552 | tf_op jit(solution)/shard_map/all_gather | solution.py:136
  352.6 92.4 %all-gather.3.cloned.1.call-done = f32[8,9,16384]{2,1,0:T(8,128)} async-done(((f32[1,9,16384]{2,1,0:T(8,128)}), f32[8,9,16384]{2,1,0:T(8,128)}) %all-gather.3.cloned.1.call-update) | async-done | bytes 4718608 | tf_op jit(solution)/shard_map/all_gather | solution.py:12
  452.7 6.5 all-reduce
  464.1 7.2 psum.53
  484.4 7.8 broadcast.107
  492.2 45.9 %while.42 = (s32[]{:T(128)}, f32[8,8,9,4096]{3,2,1,0:T(8,128)}, f32[8,8,9,64]{3,2,1,0:T(8,128)}, s32[8,8,4096]{2,1,0:T(8,128)}, s32[]{:T(128)}) while((s32[]{:T(128)}, f32[8,8,9,4096]{3,2,1,0:T(8,128)}, f32[8,8,9,64]{3,2,1,0:T(8,128)}, s32[8,8,4096]{2,1,0:T(8,128)}, s32[]{:T(128)}) %tuple.114), condition=%wide.region_24.25_spmd, body=%wide.region_23.24_spmd.sunk | while | flops 228589568 | bytes 2556993 | solution.py:66
  538.1 14.9 %copy.31 = f32[64,9,4096]{2,0,1:T(8,128)} copy(f32[64,9,4096]{2,1,0:T(8,128)} %bitcast.162) | data formatting | bytes 18874368 | tf_op jit(solution)/shard_map/mul | solution.py:77
  552.9 8.0 fusion.24
  565.6 34.1 %all-reduce.5.cloned.1.call-done = f32[3,65536]{1,0:T(4,128)} async-done(((f32[3,65536]{1,0:T(4,128)}), f32[3,65536]{1,0:T(4,128)}) %all-reduce.5.cloned.1.call-update) | async-done | bytes 786448 | tf_op jit(solution)/shard_map/psum | solution.py:144
  599.7 10.9 %add_reduce_fusion.2 = (f32[65536]{0:T(1024)}, f32[65536]{0:T(1024)}, f32[65536]{0:T(1024)S(1)}) fusion(f32[6,65536]{1,0:T(8,128)} %copy-done.7, f32[3,65536]{1,0:T(4,128)} %all-reduce.5.cloned.1.call-done), kind=kLoop, calls=%fused_computation.102 | loop fusion | flops 983040 | bytes 3145728 | tf_op jit(solution)/shard_map/add | solution.py:50
  619.2 10.6 %fusion.25 = f32[64,9,4096]{2,0,1:T(8,128)} fusion(bf16[64,2,9,4096]{3,0,2,1:T(8,128)(2,1)} %bitcast.155, f32[64,2,4096]{2,0,1:T(8,128)S(1)} %sub.46), kind=kLoop, calls=%fused_computation.43 | loop fusion | flops 11796480 | bytes 20971520 | tf_op jit(solution)/shard_map/reduce_sum | solution.py:149
  629.9 53.2 %while.43 = (s32[]{:T(128)}, f32[8,8,9,64]{3,2,1,0:T(8,128)S(1)}, f32[8,8,9,4096]{3,1,0,2:T(8,128)}, s32[8,8,4096]{2,1,0:T(8,128)}, s32[]{:T(128)}) while((s32[]{:T(128)}, f32[8,8,9,64]{3,2,1,0:T(8,128)S(1)}, f32[8,8,9,4096]{3,1,0,2:T(8,128)}, s32[8,8,4096]{2,1,0:T(8,128)}, s32[]{:T(128)}) %tuple.113), condition=%wide.region_31.32_spmd, body=%wide.region_30.31_spmd.sunk | while | flops 228589568 | bytes 3997769 | solution.py:90
  685.6 125.1 %all-gather.5.cloned.1.call-done = f32[8,9,16384]{2,1,0:T(8,128)} async-done(((f32[1,9,16384]{2,1,0:T(8,128)}), f32[8,9,16384]{2,1,0:T(8,128)}) %all-gather.5.cloned.1.call-update) | async-done | bytes 4718608 | tf_op jit(solution)/shard_map/all_gather | solution.py:12
  816.6 6.4 psum.55
  (175 shorter events, 291.3 us)
Async XLA Ops:
  7.2 194.9 %all-reduce.7.cloned.1.call-start = ((), (), s32[]{:S(2)}) async-start(), calls=%async_computation.3 | async-start | bytes 6291456 | tf_op jit(solution)/shard_map/psum | solution.py:133
  11.9 0.7 copy-start.13
  16.0 2.3 copy-start.11
  18.2 37.3 %copy-start.14 = (s32[1,1,64]{2,1,0:T(1,128)S(1)}, s32[1,1,64]{2,1,0:T(1,128)}, u32[]{:S(2)}) copy-start(s32[1,1,64]{2,1,0:T(1,128)} %param.20) | copy-start | bytes 772
  53.0 4.8 copy-start.1
  119.9 8.1 copy-start
  127.9 1.4 copy-start.2
  132.6 312.4 %all-gather.3.cloned.1.call-start = ((), (), s32[]{:S(2)}) async-start(), calls=%async_computation | async-start | bytes 9437184 | tf_op jit(solution)/shard_map/all_gather | solution.py:12
  202.0 8.7 %copy-start.9 = (f32[65536]{0:T(1024)S(1)}, f32[65536]{0:T(1024)}, u32[]{:S(2)}) copy-start(f32[65536]{0:T(1024)} %param.19) | copy-start | bytes 786436
  218.3 3.3 copy-start.10
  220.3 1.3 copy-start.7
  232.9 1.6 copy-start.3
  308.7 5.3 copy-start.12
  313.9 285.7 %all-reduce.5.cloned.1.call-start = ((), (), s32[]{:S(2)}) async-start(), calls=%async_computation.1 | async-start | bytes 2097152 | tf_op jit(solution)/shard_map/psum | solution.py:144
  560.9 1.4 copy-start.4
  565.6 245.2 %all-gather.5.cloned.1.call-start = ((), (), s32[]{:S(2)}) async-start(), calls=%async_computation.2 | async-start | bytes 9437184 | tf_op jit(solution)/shard_map/all_gather | solution.py:12
  617.4 1.6 copy-start.5
  685.6 129.1 %copy-start.6 = (f32[9,16384]{1,0:T(8,128)S(1)}, f32[9,16384]{1,0:T(8,128)}, u32[]{:S(2)}) copy-start(f32[9,16384]{1,0:T(8,128)} %all_gather.13) | copy-start | bytes 1769476
  685.6 129.1 %copy-start.8 = (f32[9,16384]{1,0:T(8,128)S(1)}, f32[9,16384]{1,0:T(8,128)}, u32[]{:S(2)}) copy-start(f32[9,16384]{1,0:T(8,128)} %multiply_add_fusion.1) | copy-start | bytes 1769476
Sparse Core Ops, SparseCore 0:
  132.7 69.2 all-reduce.6
  314.1 130.8 all-gather.2
  565.7 33.9 all-reduce.4
  685.7 124.9 all-gather.4
